TPU v7x, 32 devices: a whole 2x2x4 slice. The times are simulated.
32 devices in a mesh: grp: 2 (over y), wide: 16 (over z, x, core).
Axes of the slice: x: 2, y: 2, z: 4, core: 2. Of those that a mesh axis runs over, the one named last changes fastest.
Arguments:
- activations: bfloat16 [2, 1024, 4096], P('grp', 'wide'), parts along dimension 0, may hold values from -6 to 6
- output_grads: bfloat16 [2, 1024, 4096], P('grp', None, 'wide'), parts along dimension 0, may hold values from -0.1875 to 0.1875
- token_ids: int32 [2, 1024], P('grp'), parts along dimension 0, may hold values from 0 to 128255, as said below
- row_signs: int32 [4096], replicated, may hold values from -1 to 1, as said below
- column_signs: int32 [4096], replicated, may hold values from -1 to 1, as said below
- kept_blocks: int32 [8192], P('wide'), may hold values from 0 to 131071, as said below
- queries: bfloat16 [256, 1048576], P(None, 'wide'), may hold values from -0.0078125 to 0.0078125
Outputs:
- sketches: bfloat16 [2, 1048576], P('grp', 'wide'), parts along dimension 0
- scores: float32 [256, 2], P('wide', 'grp'), parts along dimension 1
There are 2 independent parts, one for each index of `grp`. A program takes and returns all parts, laid end to end along the dimension named above; an argument that names none is the same for every part. Nothing has to cross between parts.
Inputs may be any that keep to these rules, and one draw needn't show every extreme that they name: `token_ids`: id 0 marks padding. Each sequence ends with one run of one or more padding ids, and 512 or more of its ids are 1 or more. `row_signs`: every entry is +1 or -1. `column_signs`: every entry is +1 or -1. `kept_blocks`: A block number b names column b // 32 and rows (b % 32) * 128 up to (b % 32 + 1) * 128 - 1 of a sequence's projected matrix. For every d, entries d * 512 up to (d + 1) * 512 - 1 are distinct and name columns d * 256 up to (d + 1) * 256 - 1.
All inputs are finite; a program needn't handle non-finite values.
Results may differ from a plain program's by a relative error of at most 0.006.
Values may be sent and summed in bfloat16 or wider, within the bound.
A program may use at most 256 MiB of HBM per device.

v0:
```python
import jax
import jax.numpy as jnp
from jax import lax
from jax.sharding import PartitionSpec as P

ROWBLK = 128


def sign_table(bit_count):
    length = 2**bit_count
    indices = jnp.arange(length, dtype=jnp.int32)
    common = jnp.bitwise_and(indices[:, None], indices[None, :])
    parity = jnp.zeros((length, length), jnp.int32)
    for position in range(bit_count):
        parity = parity + jnp.bitwise_and(jnp.right_shift(common, position), 1)
    signs = 1 - 2 * jnp.bitwise_and(parity, 1)
    return (signs.astype(jnp.float32) * length ** (-0.5)).astype(jnp.bfloat16)


def hadamard_table(order_size):
    total_bits = order_size.bit_length() - 1
    low_bits = total_bits // 2
    high_table = sign_table(total_bits - low_bits)
    low_table = sign_table(low_bits)
    high_table, low_table = lax.optimization_barrier((high_table, low_table))
    return (high_table[:, None, :, None] * low_table[None, :, None, :]).reshape(
        order_size, order_size
    )


def per_device(activations, output_grads, token_ids, row_signs, column_signs, kept_blocks, queries):
    model_width = column_signs.shape[0]
    hadamard = hadamard_table(model_width)
    row_blocks = model_width // ROWBLK
    column_sign = column_signs.astype(jnp.bfloat16)
    row_sign = row_signs.astype(jnp.bfloat16)
    weight = (token_ids != 0).astype(jnp.bfloat16)
    columns_dev = output_grads.shape[2]
    device = lax.axis_index("wide")
    local_blocks = kept_blocks - device * (columns_dev * row_blocks)
    turned = jnp.einsum(
        "stj,jk->stk",
        activations * column_sign[None, None, :],
        hadamard,
        preferred_element_type=jnp.float32,
    ).astype(jnp.bfloat16)
    columns = lax.all_to_all(turned, "wide", split_axis=2, concat_axis=1, tiled=True)
    weighted = columns * weight[:, :, None]
    half_turned = jnp.einsum(
        "stc,sti->sci",
        weighted,
        lax.all_gather(output_grads, "wide", axis=2, tiled=True),
        preferred_element_type=jnp.float32,
    ).astype(jnp.bfloat16)
    signed = half_turned * row_sign[None, None, :]
    projected = jnp.einsum("scj,ji->sci", signed, hadamard, preferred_element_type=jnp.float32)
    items = projected.shape[0]
    block_rows = projected.reshape(items, projected.shape[1] * row_blocks, ROWBLK)
    picked = jnp.take(block_rows, local_blocks, axis=1)
    sketches = picked.reshape(items, picked.shape[1] * ROWBLK).astype(jnp.bfloat16)
    scores = lax.psum_scatter(
        jnp.einsum("qc,sc->qs", queries, sketches, preferred_element_type=jnp.float32),
        "wide",
        scatter_dimension=0,
        tiled=True,
    )
    return (sketches, scores)


def solution(mesh):
    placed = (
        P("grp", "wide", None),
        P("grp", None, "wide"),
        P("grp", None),
        P(),
        P(),
        P("wide"),
        P(None, "wide"),
    )
    return jax.shard_map(
        per_device,
        mesh=mesh,
        in_specs=placed,
        out_specs=(P("grp", "wide"), P("wide", "grp")),
        check_vma=False,
    )
```

profile of v0, /device:TPU:0, one launch (start us, length us, event | category | flops | bytes accessed | tf_op | source)
XLA Modules:
  0.0 292.9 jit_solution(1452810544550997973)
XLA Ops:
  7.2 0.0 all-gather.2.cloned.1.call-start
  7.2 0.7 all-gather.2.cloned.1.call-update
  7.9 21.2 %broadcast_multiply_fusion = bf16[64,64,64,64]{3,2,1,0:T(8,128)(2,1)} fusion(bf16[64,64]{1,0:T(8,128)(2,1)S(1)} %multiply_convert_fusion), kind=kLoop, calls=%fused_computation.1 | loop fusion | flops 16777216 | bytes 33562624 | tf_op jit(solution)/shard_map/mul | solution.py:26
  29.1 87.2 %mul.83 = bf16[4096,4096]{1,0:T(8,128)(2,1)} reshape(bf16[64,64,64,64]{3,2,1,0:T(8,128)(2,1)} %broadcast_multiply_fusion) | data formatting | bytes 67108864 | tf_op jit(solution)/shard_map/mul | solution.py:26
  116.3 13.6 %fusion.8 = bf16[1,64,4096]{2,1,0:T(8,128)(2,1)S(1)} fusion(bf16[4096,4096]{1,0:T(8,128)(2,1)} %mul.83, bf16[1,64,4096]{2,1,0:T(8,128)(2,1)S(1)} %copy-done, bf16[4096]{0:T(1024)(128)(2,1)S(1)} %convert_element_type.43), kind=kOutput, calls=%fused_computation.7 | convolution fusion | flops 2148007936 | bytes 34611200 | tf_op jit(solution)/shard_map/stj,jk->stk/dot_general | solution.py:41
  130.0 0.0 copy-start.2
  130.0 2.8 copy.12
  132.8 0.5 broadcast.80
  133.3 22.4 %reduce.2 = bf16[4096,64]{1,0:T(8,128)(2,1)S(1)} reduce(bf16[4096,1,64]{2,1,0:T(2,128)(2,1)S(1)} %bitcast.56, bf16[]{:T(256)} %broadcast.80), dimensions={1}, to_apply=%bitcast.47.reduce_sub_computation | reduce | bytes 1048578
  155.7 1.5 reshape.131
  157.2 7.4 %all-to-all-start = ((bf16[16,2,8192]{2,1,0:T(2,128)(2,1)}), bf16[16,2,8192]{2,1,0:T(2,128)(2,1)S(1)}, u32[]{:S(2)}, u32[]{:S(2)}) async-start(bf16[16,2,8192]{2,1,0:T(2,128)(2,1)} %reshape.131), calls=%async_computation | async-start | bytes 1048576 | tf_op jit(solution)/shard_map/all_to_all | solution.py:47
  164.7 0.2 reduce-scatter.4.cloned.1.call-start
  164.9 0.1 reshape.111
  165.0 0.1 copy.14
  165.2 0.1 broadcast_bitcast_fusion
  165.3 13.6 %all-to-all-done = bf16[16,2,8192]{2,1,0:T(2,128)(2,1)S(1)} async-done(((bf16[16,2,8192]{2,1,0:T(2,128)(2,1)}), bf16[16,2,8192]{2,1,0:T(2,128)(2,1)S(1)}, u32[]{:S(2)}, u32[]{:S(2)}) %all-to-all-start) | async-done | bytes 524320 | tf_op jit(solution)/shard_map/all_to_all | solution.py:47
  178.9 1.2 reshape.132
  180.2 2.3 copy.13
  182.5 0.1 copy.19
  182.6 0.2 fusion.13
  182.8 0.2 copy.15
  182.9 0.0 all-gather.2.cloned.1.call-done
  183.0 22.9 %fusion.10 = f32[256,4096]{1,0:T(8,128)} fusion(bf16[4096,4096]{1,0:T(8,128)(2,1)} %mul.83, bf16[1024,256]{1,0:T(8,128)(2,1)S(1)} %bitcast.60, bf16[1,1024,4096]{2,1,0:T(8,128)(2,1)} %all-gather.2.cloned.1.call-done, bf16[4096]{0:T(1024)(128)(2,1)S(1)} %convert_element_type.49), kind=kOutput, calls=%fused_computation.8 | convolution fusion | flops 10739515392 | bytes 46669824 | tf_op jit(solution)/shard_map/scj,ji->sci/dot_general | solution.py:56
  205.9 4.9 %reshape.112 = f32[8192,128]{1,0:T(8,128)} reshape(f32[256,4096]{1,0:T(8,128)} %fusion.10) | data formatting | bytes 8388608 | tf_op jit(solution)/shard_map/reshape | solution.py:58
  210.8 3.2 %gather_fusion = f32[512,128]{1,0:T(8,128)S(1)} fusion(f32[8192,128]{1,0:T(8,128)} %reshape.112, s32[1024]{0:T(1024)S(1)} %pad_clamp_fusion), kind=kCustom, calls=%fused_computation | custom fusion | bytes 526336 | tf_op jit(solution)/shard_map/jit(_take)/gather | solution.py:59
  214.1 0.1 fusion.17
  214.2 0.1 reshape.126
  214.3 15.1 %convolution_bitcast_fusion = f32[256,1]{1,0:T(8,128)} fusion(bf16[65536,1]{0,1:T(2,128)(2,1)S(1)} %reshape.126, bf16[256,65536]{1,0:T(8,128)(2,1)} %param.13), kind=kOutput, calls=%fused_computation.9 | convolution fusion | flops 33554432 | bytes 33686528 | tf_op jit(solution)/shard_map/qc,sc->qs/dot_general | solution.py:62
  229.4 0.0 reduce-scatter.4.cloned.1.call-update
  229.5 1.1 fusion.16
  230.6 54.2 %reduce-scatter.4.cloned.1.call-done = f32[16,1]{1,0:T(8,128)} async-done(((f32[256,1]{1,0:T(8,128)}), f32[16,1]{1,0:T(8,128)}) %reduce-scatter.4.cloned.1.call-update) | async-done | bytes 80
  284.8 1.3 copy.17
  (15 shorter events, 0.1 us)
Async XLA Ops:
  7.2 175.8 %all-gather.2.cloned.1.call-start = ((), (), s32[]{:S(2)}) async-start(), calls=%async_computation.2 | async-start | bytes 8912896 | tf_op jit(solution)/shard_map/all_gather | solution.py:52
  29.1 87.2 %copy-start.1 = (s32[4096]{0:T(1024)S(1)}, s32[4096]{0:T(1024)}, u32[]{:S(2)}) copy-start(s32[4096]{0:T(1024)} %param.11) | copy-start | bytes 49156
  29.1 87.2 %copy-start = (bf16[1,64,4096]{2,1,0:T(8,128)(2,1)S(1)}, bf16[1,64,4096]{2,1,0:T(8,128)(2,1)}, u32[]{:S(2)}) copy-start(bf16[1,64,4096]{2,1,0:T(8,128)(2,1)} %param.7) | copy-start | bytes 1572868
  130.0 34.9 %copy-start.3 = (s32[1,1024]{1,0:T(1,128)S(1)}, s32[1,1024]{1,0:T(1,128)}, u32[]{:S(2)}) copy-start(s32[1,1024]{1,0:T(1,128)} %param.9) | copy-start | bytes 12292
  130.0 35.2 %copy-start.2 = (s32[4096]{0:T(1024)S(1)}, s32[4096]{0:T(1024)}, u32[]{:S(2)}) copy-start(s32[4096]{0:T(1024)} %param.10) | copy-start | bytes 49156
  130.0 35.2 %copy-start.4 = (s32[512]{0:T(512)S(1)}, s32[512]{0:T(512)}, u32[]{:S(2)}) copy-start(s32[512]{0:T(512)} %param.12) | copy-start | bytes 6148
  157.2 21.7 %all-to-all-start = ((bf16[16,2,8192]{2,1,0:T(2,128)(2,1)}), bf16[16,2,8192]{2,1,0:T(2,128)(2,1)S(1)}, u32[]{:S(2)}, u32[]{:S(2)}) async-start(bf16[16,2,8192]{2,1,0:T(2,128)(2,1)} %reshape.131), calls=%async_computation | async-start | bytes 1048576 | tf_op jit(solution)/shard_map/all_to_all | solution.py:47
  164.7 120.1 %reduce-scatter.4.cloned.1.call-start = ((), (), s32[]{:S(2)}) async-start(), calls=%async_computation.3 | async-start | bytes 139264
Sparse Core Ops, SparseCore 0:
  10.1 80.4 all-gather.1
  229.6 55.1 reduce-scatter.3
where the time goes:
time: 296 us; the launch traced here: 293 us
  local copies, waits for them, and re-layouts  106 us (36%)
  waiting for transfers between devices  68.6 us (23%)
  matrix products  51.7 us (17%)
  other arithmetic  45.1 us (15%)
  between operations  14.2 us (5%)
  starting transfers between devices  7.7 us (3%)
    mul x1, local copies, waits for them, and re-layouts, hadamard_table(): high_table[:, None, :, None] * low_table[None, :, None, :]  87.2 us
    unnamed x3, waiting for transfers between devices  54.9 us
    dot_general x1, matrix products, per_device(): jnp.einsum('scj,ji->sci', signed, hadamard, preferred_element_type=jnp.fl...  22.9 us
    unnamed x1, other arithmetic  22.4 us
    mul x1, other arithmetic, hadamard_table(): high_table[:, None, :, None] * low_table[None, :, None, :]  21.2 us
    dot_general x1, matrix products, per_device(): jnp.einsum('qc,sc->qs', queries, sketches, preferred_element_type=jnp.flo...  15.1 us
    dot_general x1, matrix products, per_device(): jnp.einsum('stj,jk->stk', activations * column_sign[None, None, :], hadam...  13.6 us
    all_to_all x1, waiting for transfers between devices, per_device(): lax.all_to_all(turned, 'wide', split_axis=2, concat_axis=1, tiled=True)  13.6 us
  transfers between devices with their start and end apart: 3, of which 2 were waited for; matrix products, arithmetic and copies ran while one was open for 53% of the time, Pallas kernels for 0%

commit v1 on v0

--- a/solution.py
+++ b/solution.py
@@ -1,9 +1,25 @@
+import functools
 import jax
 import jax.numpy as jnp
 from jax import lax
 from jax.sharding import PartitionSpec as P
 
 ROWBLK = 128
+
+
+def view_detail(sheet, where_dim, join_dim):
+    return jnp.concatenate(
+        lax.all_to_all(
+            jnp.stack(jnp.split(sheet, lax.axis_size("wide"), axis=join_dim)),
+            axis_name="wide",
+            split_axis=0,
+            concat_axis=0,
+        ),
+        axis=where_dim,
+    )
+
+
+waves_do = functools.partial(view_detail, where_dim=1, join_dim=2)
 
 
 def sign_table(bit_count):
@@ -44,7 +60,7 @@
         hadamard,
         preferred_element_type=jnp.float32,
     ).astype(jnp.bfloat16)
-    columns = lax.all_to_all(turned, "wide", split_axis=2, concat_axis=1, tiled=True)
+    columns = waves_do(turned)
     weighted = columns * weight[:, :, None]
     half_turned = jnp.einsum(
         "stc,sti->sci",

time: 296 us -> 274 us (0.926)
  other arithmetic: 45.1 us -> 22.7 us
    unnamed x1 -> x0, other arithmetic: 22.4 us -> none
    unnamed x16 -> x27, local copies, waits for them, and re-layouts: 4.79 us -> 10.7 us
  transfers between devices with their start and end apart: 3 -> 3, of which waited for: 2 -> 2; matrix products, arithmetic and copies ran while one was open for 53% -> 49% of each run, Pallas kernels for 0% -> 0%
where the time goes in v1:
time: 274 us; the launch traced here: 272 us
  local copies, waits for them, and re-layouts  107 us (39%)
  waiting for transfers between devices  68.7 us (25%)
  matrix products  51.7 us (19%)
  other arithmetic  22.7 us (8%)
  between operations  14.2 us (5%)
  starting transfers between devices  7.7 us (3%)
    mul x1, local copies, waits for them, and re-layouts, hadamard_table(): high_table[:, None, :, None] * low_table[None, :, None, :]  87.2 us
    unnamed x3, waiting for transfers between devices  55 us
    dot_general x1, matrix products, per_device(): jnp.einsum('scj,ji->sci', signed, hadamard, preferred_element_type=jnp.fl...  22.9 us
    mul x1, other arithmetic, hadamard_table(): high_table[:, None, :, None] * low_table[None, :, None, :]  21.2 us
    dot_general x1, matrix products, per_device(): jnp.einsum('qc,sc->qs', queries, sketches, preferred_element_type=jnp.flo...  15.1 us
    all_to_all x1, waiting for transfers between devices, view_detail(): lax.all_to_all(jnp.stack(jnp.split(sheet, lax.axis_size('wide'), axis=joi...  13.7 us
    dot_general x1, matrix products, per_device(): jnp.einsum('stj,jk->stk', activations * column_sign[None, None, :], hadam...  13.6 us
    unnamed x27, local copies, waits for them, and re-layouts  10.7 us
  transfers between devices with their start and end apart: 3, of which 2 were waited for; matrix products, arithmetic and copies ran while one was open for 49% of the time, Pallas kernels for 0%

profile of v1, /device:TPU:0, one launch (start us, length us, event | category | flops | bytes accessed | tf_op | source)
XLA Modules:
  0.0 271.7 jit_solution(11914816879175366050)
XLA Ops:
  7.2 0.7 all-gather.2.cloned.1.call-update
  7.9 21.2 %broadcast_multiply_fusion = bf16[64,64,64,64]{3,2,1,0:T(8,128)(2,1)} fusion(bf16[64,64]{1,0:T(8,128)(2,1)S(1)} %multiply_convert_fusion), kind=kLoop, calls=%fused_computation.1 | loop fusion | flops 16777216 | bytes 33562624 | tf_op jit(solution)/shard_map/mul | solution.py:42
  29.1 87.2 %mul.83 = bf16[4096,4096]{1,0:T(8,128)(2,1)} reshape(bf16[64,64,64,64]{3,2,1,0:T(8,128)(2,1)} %broadcast_multiply_fusion) | data formatting | bytes 67108864 | tf_op jit(solution)/shard_map/mul | solution.py:42
  116.3 13.6 %fusion.8 = bf16[1,64,4096]{2,1,0:T(8,128)(2,1)S(1)} fusion(bf16[4096,4096]{1,0:T(8,128)(2,1)} %mul.83, bf16[1,64,4096]{2,1,0:T(8,128)(2,1)S(1)} %copy-done, bf16[4096]{0:T(1024)(128)(2,1)S(1)} %convert_element_type.43), kind=kOutput, calls=%fused_computation.7 | convolution fusion | flops 2148007936 | bytes 34611200 | tf_op jit(solution)/shard_map/stj,jk->stk/dot_general | solution.py:57
  130.0 0.6 fusion.33
  130.6 0.6 fusion.32
  131.2 0.6 fusion.31
  131.8 0.6 fusion.30
  132.4 0.6 fusion.29
  133.1 0.6 fusion.28
  133.7 0.6 fusion.27
  134.3 0.6 fusion.26
  134.9 0.6 fusion.25
  135.5 0.6 fusion.24
  136.1 0.6 fusion.23
  136.7 0.6 fusion.22
  137.4 0.6 fusion.21
  138.0 0.6 fusion.20
  138.6 0.6 fusion.19
  139.2 0.6 fusion.18
  139.8 7.4 %all-to-all-start = ((bf16[16,1,64,256]{3,2,1,0:T(8,128)(2,1)}), bf16[16,1,64,256]{3,2,1,0:T(8,128)(2,1)S(1)}, u32[]{:S(2)}, u32[]{:S(2)}) async-start(bf16[16,1,64,256]{3,2,1,0:T(8,128)(2,1)} %fusion.18), calls=%async_computation | async-start | bytes 1048576 | tf_op jit(solution)/shard_map/all_to_all | solution.py:12
  147.3 0.2 reduce-scatter.4.cloned.1.call-start
  147.8 13.7 %all-to-all-done = bf16[16,1,64,256]{3,2,1,0:T(8,128)(2,1)S(1)} async-done(((bf16[16,1,64,256]{3,2,1,0:T(8,128)(2,1)}), bf16[16,1,64,256]{3,2,1,0:T(8,128)(2,1)S(1)}, u32[]{:S(2)}, u32[]{:S(2)}) %all-to-all-start) | async-done | bytes 524320 | tf_op jit(solution)/shard_map/all_to_all | solution.py:12
  161.6 0.2 broadcast_multiply_fusion.1
  161.8 22.9 %fusion.10 = f32[256,4096]{1,0:T(8,128)} fusion(bf16[4096,4096]{1,0:T(8,128)(2,1)} %mul.83, bf16[1024,256]{1,0:T(8,128)(2,1)S(1)} %bitcast.106, bf16[1,1024,4096]{2,1,0:T(8,128)(2,1)} %all-gather.2.cloned.1.call-done, bf16[4096]{0:T(1024)(128)(2,1)S(1)} %convert_element_type.49), kind=kOutput, calls=%fused_computation.8 | convolution fusion | flops 10739515392 | bytes 46669824 | tf_op jit(solution)/shard_map/scj,ji->sci/dot_general | solution.py:72
  184.7 4.9 %reshape.113 = f32[8192,128]{1,0:T(8,128)} reshape(f32[256,4096]{1,0:T(8,128)} %fusion.10) | data formatting | bytes 8388608 | tf_op jit(solution)/shard_map/reshape | solution.py:74
  189.6 3.2 %gather_fusion = f32[512,128]{1,0:T(8,128)S(1)} fusion(f32[8192,128]{1,0:T(8,128)} %reshape.113, s32[1024]{0:T(1024)S(1)} %pad_clamp_fusion), kind=kCustom, calls=%fused_computation | custom fusion | bytes 526336 | tf_op jit(solution)/shard_map/jit(_take)/gather | solution.py:75
  193.0 0.1 reshape.127
  193.1 15.1 %convolution_bitcast_fusion = f32[256,1]{1,0:T(8,128)} fusion(bf16[65536,1]{0,1:T(2,128)(2,1)S(1)} %reshape.127, bf16[256,65536]{1,0:T(8,128)(2,1)} %param.13), kind=kOutput, calls=%fused_computation.9 | convolution fusion | flops 33554432 | bytes 33686528 | tf_op jit(solution)/shard_map/qc,sc->qs/dot_general | solution.py:78
  208.3 1.1 fusion.15
  209.4 54.3 %reduce-scatter.4.cloned.1.call-done = f32[16,1]{1,0:T(8,128)} async-done(((f32[256,1]{1,0:T(8,128)}), f32[16,1]{1,0:T(8,128)}) %reduce-scatter.4.cloned.1.call-update) | async-done | bytes 80
  263.6 1.3 copy.10
  (22 shorter events, 0.5 us)
Async XLA Ops:
  7.2 154.6 %all-gather.2.cloned.1.call-start = ((), (), s32[]{:S(2)}) async-start(), calls=%async_computation.2 | async-start | bytes 8912896 | tf_op jit(solution)/shard_map/all_gather | solution.py:68
  29.1 87.2 %copy-start.1 = (s32[4096]{0:T(1024)S(1)}, s32[4096]{0:T(1024)}, u32[]{:S(2)}) copy-start(s32[4096]{0:T(1024)} %param.11) | copy-start | bytes 49156
  29.1 87.2 %copy-start = (bf16[1,64,4096]{2,1,0:T(8,128)(2,1)S(1)}, bf16[1,64,4096]{2,1,0:T(8,128)(2,1)}, u32[]{:S(2)}) copy-start(bf16[1,64,4096]{2,1,0:T(8,128)(2,1)} %param.7) | copy-start | bytes 1572868
  116.3 31.2 %copy-start.3 = (s32[1,1024]{1,0:T(1,128)S(1)}, s32[1,1024]{1,0:T(1,128)}, u32[]{:S(2)}) copy-start(s32[1,1024]{1,0:T(1,128)} %param.9) | copy-start | bytes 12292
  116.3 31.3 %copy-start.2 = (s32[4096]{0:T(1024)S(1)}, s32[4096]{0:T(1024)}, u32[]{:S(2)}) copy-start(s32[4096]{0:T(1024)} %param.10) | copy-start | bytes 49156
  116.3 31.4 %copy-start.4 = (s32[512]{0:T(512)S(1)}, s32[512]{0:T(512)}, u32[]{:S(2)}) copy-start(s32[512]{0:T(512)} %param.12) | copy-start | bytes 6148
  139.8 21.7 %all-to-all-start = ((bf16[16,1,64,256]{3,2,1,0:T(8,128)(2,1)}), bf16[16,1,64,256]{3,2,1,0:T(8,128)(2,1)S(1)}, u32[]{:S(2)}, u32[]{:S(2)}) async-start(bf16[16,1,64,256]{3,2,1,0:T(8,128)(2,1)} %fusion.18), calls=%async_computation | async-start | bytes 1048576 | tf_op jit(solution)/shard_map/all_to_all | solution.py:12
  147.3 116.3 %reduce-scatter.4.cloned.1.call-start = ((), (), s32[]{:S(2)}) async-start(), calls=%async_computation.3 | async-start | bytes 139264
Sparse Core Ops, SparseCore 0:
  10.1 80.4 all-gather.1
  208.4 55.1 reduce-scatter.3
